TPU v7x, 128 devices: a whole 4x4x4 slice. The times are simulated.
128 devices in a mesh: seg: 4 (over z_lo, core), batch: 32 (over z_hi, y, x).
Axes of the slice: x: 4, y: 4, z: 4 (z_hi: 2, z_lo: 2; z = z_hi * 2 + z_lo), core: 2. Of those that a mesh axis runs over, the one named last changes fastest.
Arguments:
- starts: float32 [4, 4096, 1024], P('seg', 'batch'), may hold values from -6 to 6
- targets: float32 [4, 4096, 1024], P('seg', 'batch'), may hold values from -6 to 6
- counts: int32 [4], P('seg'), may hold values from 1 to 3, as said below
- w_in: bfloat16 [1024, 1024], P('batch'), may hold values from -0.1875 to 0.1875
- b_in: float32 [1024], replicated, may hold values from -3 to 3
- w_out: bfloat16 [1024, 1024], P('batch'), may hold values from -0.1875 to 0.1875
Outputs:
- grad_starts: float32 [4, 4096, 1024], P('seg', 'batch')
- grad_w_in: float32 [1024, 1024], P('batch')
- grad_w_out: float32 [1024, 1024], P('batch')
- grad_b_in: float32 [1024], P('batch')
Inputs may be any that keep to these rules, and one draw needn't show every extreme that they name: `counts`: some segment takes 3 steps and some takes 1.
All inputs are finite; a program needn't handle non-finite values.
Results may differ from a plain program's by a relative error of at most 0.00125.
Values may be sent and summed in bfloat16 or wider, within the bound.
No kernel may reach another device: no remote copies, remote signals or barrier semaphores. Data moves between devices by JAX's collectives and lax.ppermute only.
A program may use at most 64 MiB of HBM per device.

v0:
```python
import math
import jax
import jax.numpy as jnp
from jax import lax
from jax.sharding import PartitionSpec as P

D = 1024
MAXSTEP = 3
time_step = 0.25
penalty = 1.0


def shifted(block, axis, distance):
    devices = range(lax.axis_size(axis))
    route = [(i - distance, i) for i in devices if i - distance in devices]
    return lax.ppermute(block, axis, route)


def contract_rows(left, right):
    return lax.dot_general(
        left, right, (((0,), (0,)), ((), ())), preferred_element_type=jnp.float32
    )


def contract_cols(left, right):
    return lax.dot_general(
        left, right, (((1,), (1,)), ((), ())), preferred_element_type=jnp.float32
    )


def vector_field(current, w_in, b_in, w_out):
    inputs = current.astype(jnp.bfloat16)
    hidden = jnp.tanh(jnp.dot(inputs, w_in, preferred_element_type=jnp.float32) + b_in)
    slope = jnp.dot(hidden.astype(jnp.bfloat16), w_out, preferred_element_type=jnp.float32)
    return (slope, inputs, hidden)


def runge_kutta(current, w_in, b_in, w_out):
    slope_one, in_one, hid_one = vector_field(current, w_in, b_in, w_out)
    slope_two, in_two, hid_two = vector_field(
        current + 0.5 * time_step * slope_one, w_in, b_in, w_out
    )
    slope_three, in_three, hid_three = vector_field(
        current + 0.5 * time_step * slope_two, w_in, b_in, w_out
    )
    slope_four, in_four, hid_four = vector_field(
        current + time_step * slope_three, w_in, b_in, w_out
    )
    updated = current + time_step / 6.0 * (
        slope_one + 2.0 * slope_two + 2.0 * slope_three + slope_four
    )
    inputs = jnp.stack([in_one, in_two, in_three, in_four])
    hiddens = jnp.stack([hid_one, hid_two, hid_three, hid_four])
    return (updated, inputs, hiddens)


def field_back(hidden, outer, w_in, w_out):
    outer_low = outer.astype(jnp.bfloat16)
    inner = contract_cols(outer_low, w_out) * (1.0 - hidden * hidden)
    inner_low = inner.astype(jnp.bfloat16)
    return (contract_cols(inner_low, w_in), outer_low, inner_low, jnp.sum(inner, axis=0))


def runge_kutta_back(state_bar, inputs, hiddens, w_in, w_out):
    back_four, outer_four, inner_four, bias_four = field_back(
        hiddens[3], time_step / 6.0 * state_bar, w_in, w_out
    )
    back_three, outer_three, inner_three, bias_three = field_back(
        hiddens[2], time_step / 3.0 * state_bar + time_step * back_four, w_in, w_out
    )
    back_two, outer_two, inner_two, bias_two = field_back(
        hiddens[1], time_step / 3.0 * state_bar + 0.5 * time_step * back_three, w_in, w_out
    )
    back_one, outer_one, inner_one, bias_one = field_back(
        hiddens[0], time_step / 6.0 * state_bar + 0.5 * time_step * back_two, w_in, w_out
    )
    new_bar = state_bar + back_one + back_two + back_three + back_four
    outers = jnp.concatenate([outer_one, outer_two, outer_three, outer_four], axis=0)
    inners = jnp.concatenate([inner_one, inner_two, inner_three, inner_four], axis=0)
    flat_inputs = inputs.reshape(-1, inputs.shape[-1])
    flat_hidden = hiddens.astype(jnp.bfloat16).reshape(-1, hiddens.shape[-1])
    grad_in_step = contract_rows(flat_inputs, inners)
    grad_out_step = contract_rows(flat_hidden, outers)
    grad_bias_step = bias_one + bias_two + bias_three + bias_four
    return (new_bar, grad_in_step, grad_out_step, grad_bias_step)


def body(starts, targets, counts, w_in, b_in, w_out):
    full_in, full_out = (
        lax.all_gather(w_in, "batch", axis=0, tiled=True),
        lax.all_gather(w_out, "batch", axis=0, tiled=True),
    )
    start_now = starts[0]
    target_now = targets[0]
    step_total = counts[0]
    seg_place = lax.axis_index("seg")
    batch_count = lax.axis_size("batch")
    row_count = start_now.shape[0]

    def advance_plain(step_index, carry):
        current, saved = carry
        saved = lax.dynamic_update_index_in_dim(saved, current, step_index, 0)
        updated, inputs, hiddens = runge_kutta(current, full_in, b_in, full_out)
        return (updated, saved)

    saved_empty = jnp.zeros((MAXSTEP, row_count, D), jnp.float32)
    end_state, saved = lax.fori_loop(0, step_total, advance_plain, (start_now, saved_empty))

    def recall(step_index):
        current = lax.dynamic_index_in_dim(saved, step_index, 0, keepdims=False)
        updated, inputs, hiddens = runge_kutta(current, full_in, b_in, full_out)
        return (inputs, hiddens)

    miss = end_state - target_now
    previous = shifted(end_state, "seg", 1)
    has_prev = (seg_place > 0).astype(jnp.float32)
    gap_here = (previous - start_now) * has_prev
    returned = shifted(penalty * gap_here, "seg", -1)
    end_bar = miss + returned

    def retreat(turn, carry):
        state_bar, acc_in, acc_out, acc_bias = carry
        step_index = step_total - 1 - turn
        inputs, hiddens = recall(step_index)
        new_bar, grad_in_step, grad_out_step, grad_bias_step = runge_kutta_back(
            state_bar, inputs, hiddens, full_in, full_out
        )
        return (new_bar, acc_in + grad_in_step, acc_out + grad_out_step, acc_bias + grad_bias_step)

    initial = (
        end_bar,
        jnp.zeros(full_in.shape, jnp.float32),
        jnp.zeros(full_out.shape, jnp.float32),
        jnp.zeros(b_in.shape, jnp.float32),
    )
    start_bar, total_in, total_out, total_bias = lax.fori_loop(0, step_total, retreat, initial)
    start_term = -(penalty * gap_here)
    grad_starts = (start_bar + start_term)[None]
    scale = 1.0 / math.sqrt(row_count * batch_count)
    scaled_in = total_in * scale
    scaled_out = total_out * scale
    scaled_bias = total_bias * scale
    shares = (
        lax.psum_scatter(scaled_in, "batch", scatter_dimension=0, tiled=True),
        lax.psum_scatter(scaled_out, "batch", scatter_dimension=0, tiled=True),
        lax.psum_scatter(scaled_bias, "batch", scatter_dimension=0, tiled=True),
    )
    grad_in, grad_out, grad_bias = lax.psum((shares[0], shares[1], shares[2]), "seg")
    return (grad_starts, grad_in, grad_out, grad_bias)


def solution(mesh):
    return jax.shard_map(
        body,
        mesh=mesh,
        in_specs=(
            P("seg", "batch", None),
            P("seg", "batch", None),
            P("seg"),
            P("batch", None),
            P(),
            P("batch", None),
        ),
        out_specs=(P("seg", "batch", None), P("batch", None), P("batch", None), P("batch")),
        check_vma=False,
    )
```

profile of v0, /device:TPU:1, one launch (start us, length us, event | category | flops | bytes accessed | tf_op | source)
XLA Modules:
  0.0 728.3 jit_solution(12884548266842338025)
XLA Ops:
  8.7 1.9 copy.12
  10.6 73.6 %all-gather.3.cloned.1.call-done = bf16[1024,1024]{1,0:T(8,128)(2,1)} async-done(((bf16[32,1024]{1,0:T(8,128)(2,1)}), bf16[1024,1024]{1,0:T(8,128)(2,1)}) %all-gather.3.cloned.1.call-update) | async-done | bytes 2097168 | tf_op jit(solution)/shard_map/all_gather | solution.py:90
  84.2 71.7 %all-gather.5.cloned.1.call-done = bf16[1024,1024]{1,0:T(8,128)(2,1)} async-done(((bf16[32,1024]{1,0:T(8,128)(2,1)}), bf16[1024,1024]{1,0:T(8,128)(2,1)}) %all-gather.5.cloned.1.call-update) | async-done | bytes 2097168 | tf_op jit(solution)/shard_map/all_gather | solution.py:91
  155.9 1.4 broadcast_in_dim.14
  157.2 16.5 %while.30 = (s32[]{:T(128)}, f32[128,1024]{1,0:T(8,128)}, f32[3,128,1024]{2,1,0:T(8,128)}, s32[]{:T(128)}, bf16[1024,1024]{1,0:T(8,128)(2,1)}, /*index=5*/f32[10...) while((s32[]{:T(128)}, f32[128,1024]{1,0:T(8,128)}, f32[3,128,1024]{2,1,0:T(8,128)}, ...), condition=%wide.region_1.2_spmd, body=%wide.region_0.1_spmd.sunk | while | flops 2150760448 | bytes 34095276 | solution.py:107
  158.9 3.1 fusion.174
  162.1 3.2 fusion.175
  165.2 3.3 fusion.176
  169.4 3.6 fusion.177
  173.7 36.4 %collective-permute-start = (f32[128,1024]{1,0:T(8,128)}, f32[128,1024]{1,0:T(8,128)S(1)}, u32[]{:S(2)}, u32[]{:S(2)}) collective-permute-start(f32[128,1024]{1,0:T(8,128)} %get-tuple-element.170), channel_id=1, source_target_pairs={{0,32},{32,64},{64,96},{1,33},{33,65},{65,97},{2,34},{34,66},{66,9... | collective-permute-start | bytes 1572872 | tf_op jit(solution)/shard_map/ppermute | solution.py:16
  210.2 6.4 collective-permute-done
  217.7 1.9 collective-permute-start.1
  220.3 8.6 %collective-permute-done.1 = f32[128,1024]{1,0:T(8,128)S(1)} collective-permute-done((f32[128,1024]{1,0:T(8,128)S(1)}, f32[128,1024]{1,0:T(8,128)S(1)}, u32[]{:S(2)}, u32[]{:S(2)}) %collective-permute-start.1) | collective-permute-done | bytes 524320 | tf_op jit(solution)/shard_map/ppermute | solution.py:16
  228.8 1.3 fusion.66
  230.1 2.5 broadcast.45.clone
  232.6 2.5 broadcast.45
  235.1 21.9 %while.31 = (s32[]{:T(128)}, f32[128,1024]{1,0:T(8,128)S(1)}, f32[1024,1024]{1,0:T(8,128)}, f32[1024,1024]{1,0:T(8,128)}, f32[1024]{0:T(1024)S(1)}, /*index=5*/s...) while((s32[]{:T(128)}, f32[128,1024]{1,0:T(8,128)S(1)}, ...), condition=%wide.region_7.8_spmd, body=%wide.region_2.7_spmd.sunk | while | flops 6195249152 | bytes 161800576 | solution.py:136
  236.1 1.2 dynamic-slice_convert_fusion.2
  237.3 1.5 fusion.211
  249.1 1.2 copy-done.5
  250.3 1.4 convolution_add_fusion.14
  252.5 1.4 convolution_add_fusion.15
  254.4 2.0 copy-done.4
  257.1 5.0 broadcast_multiply_fusion.1
  262.1 5.0 broadcast_multiply_fusion
  269.0 80.0 %all-reduce = f32[1024]{0:T(1024)S(1)} all-reduce(f32[1024]{0:T(1024)S(1)} %broadcast_multiply_fusion.2), channel_id=4, replica_groups=mesh['seg'=4,'batch'=32] {'batch'}, use_global_device_ids=true, to_apply=%region_12.13.clone | all-reduce | flops 1024 | bytes 8192
  349.1 58.6 %psum.23 = f32[32]{0:T(128)} all-reduce(f32[32]{0:T(128)S(1)} %dynamic-slice.1), channel_id=1, replica_groups=mesh['seg'=4,'batch'=32] {'seg'}, use_global_device_ids=true, to_apply=%region_13.14 | all-reduce | flops 32 | bytes 256 | tf_op jit(solution)/shard_map/psum | solution.py:148
  407.7 63.2 %reduce-scatter.3.cloned.1.call-done = f32[32,1024]{1,0:T(8,128)} async-done(((f32[1024,1024]{1,0:T(8,128)}), f32[32,1024]{1,0:T(8,128)}) %reduce-scatter.3.cloned.1.call-update) | async-done | bytes 131088 | tf_op jit(solution)/shard_map/reduce_scatter | solution.py:144
  470.9 190.8 %reduce-scatter.5.cloned.1.call-done = f32[32,1024]{1,0:T(8,128)} async-done(((f32[1024,1024]{1,0:T(8,128)}), f32[32,1024]{1,0:T(8,128)}) %reduce-scatter.5.cloned.1.call-update) | async-done | bytes 131088 | tf_op jit(solution)/shard_map/reduce_scatter | solution.py:145
  662.6 56.0 %all-reduce.4.cloned.1.call-done = (f32[32,1024]{1,0:T(8,128)}, f32[32,1024]{1,0:T(8,128)}) async-done(((f32[32,1024]{1,0:T(8,128)}, f32[32,1024]{1,0:T(8,128)}), (f32[32,1024]{1,0:T(8,128)}, f32[32,1024]{1,0:T(8,128)})) %all-reduce.4.cloned.1.call-update) | async-done | bytes 262160 | tf_op jit(solution)/shard_map/psum | solution.py:148
  718.6 1.6 copy.40
  720.2 1.6 copy.41
  (56 shorter events, 18.1 us)
Async XLA Ops:
  7.2 150.0 %copy-start.8 = (f32[1024]{0:T(1024)S(1)}, f32[1024]{0:T(1024)}, u32[]{:S(2)}) copy-start(f32[1024]{0:T(1024)} %param.14) | copy-start | bytes 12292
  7.2 77.0 %all-gather.3.cloned.1.call-start = ((), (), s32[]{:S(2)}) async-start(), calls=%async_computation.2 | async-start | bytes 2162688 | tf_op jit(solution)/shard_map/all_gather | solution.py:90
  7.9 147.9 %all-gather.5.cloned.1.call-start = ((), (), s32[]{:S(2)}) async-start(), calls=%async_computation.3 | async-start | bytes 2162688 | tf_op jit(solution)/shard_map/all_gather | solution.py:91
  8.7 462.2 %reduce-scatter.3.cloned.1.call-start = ((), (), s32[]{:S(2)}) async-start(), calls=%async_computation.4 | async-start | bytes 4325376 | tf_op jit(solution)/shard_map/reduce_scatter | solution.py:144
  158.9 3.1 copy-start
  173.7 42.9 %collective-permute-start = (f32[128,1024]{1,0:T(8,128)}, f32[128,1024]{1,0:T(8,128)S(1)}, u32[]{:S(2)}, u32[]{:S(2)}) collective-permute-start(f32[128,1024]{1,0:T(8,128)} %get-tuple-element.170), channel_id=1, source_target_pairs={{0,32},{32,64},{64,96},{1,33},{33,65},{65,97},{2,34},{34,66},{66,9... | collective-permute-start | bytes 1572872 | tf_op jit(solution)/shard_map/ppermute | solution.py:16
  217.7 11.1 %collective-permute-start.1 = (f32[128,1024]{1,0:T(8,128)S(1)}, f32[128,1024]{1,0:T(8,128)S(1)}, u32[]{:S(2)}, u32[]{:S(2)}) collective-permute-start(f32[128,1024]{1,0:T(8,128)S(1)} %subtract_multiply_fusion), channel_id=1, source_target_pairs={{32,0},{64,32},{96,64},{33,1},{65,33},{97,65},{34,2},{66,34},{98,6... | collective-permute-start | bytes 1572872 | tf_op jit(solution)/shard_map/ppermute | solution.py:16
  232.6 2.5 copy-start.1
  236.0 2.8 copy-start.2
  236.0 2.8 copy-start.7
  248.1 2.2 copy-start.5
  250.3 2.2 copy-start.3
  252.5 2.0 copy-start.6
  254.4 2.0 copy-start.4
  262.1 399.6 %reduce-scatter.5.cloned.1.call-start = ((), (), s32[]{:S(2)}) async-start(), calls=%async_computation.5 | async-start | bytes 4325376 | tf_op jit(solution)/shard_map/reduce_scatter | solution.py:145
  267.1 0.7 copy-start.9
  267.1 451.5 %all-reduce.4.cloned.1.call-start = ((), (), s32[]{:S(2)}) async-start(), calls=%async_computation.6 | async-start | bytes 524288 | tf_op jit(solution)/shard_map/psum | solution.py:148
Sparse Core Ops, SparseCore 0:
  11.1 73.0 all-gather.2
  87.3 68.5 all-gather.4
  262.2 208.6 reduce-scatter.2
  473.1 188.5 reduce-scatter.4
  664.1 54.4 all-reduce.3
where the time goes:
time: 729 us; the launch traced here: 728 us
  waiting for transfers between devices  472 us (65%)
  blocking collectives  139 us (19%)
  starting transfers between devices  38.6 us (5%)
  matrix products  27.3 us (4%)
  local copies, waits for them, and re-layouts  20.2 us (3%)
  between operations  15.2 us (2%)
  other arithmetic  13.7 us (2%)
    reduce_scatter x1, waiting for transfers between devices, body(): lax.psum_scatter(scaled_out, 'batch', scatter_dimension=0, tiled=True)  191 us
    unnamed x1, blocking collectives  80 us
    all_gather x1, waiting for transfers between devices, body(): lax.all_gather(w_in, 'batch', axis=0, tiled=True)  73.6 us
    all_gather x1, waiting for transfers between devices, body(): lax.all_gather(w_out, 'batch', axis=0, tiled=True)  71.7 us
    reduce_scatter x1, waiting for transfers between devices, body(): lax.psum_scatter(scaled_in, 'batch', scatter_dimension=0, tiled=True)  63.2 us
    psum x1, blocking collectives, body(): lax.psum((shares[0], shares[1], shares[2]), 'seg')  58.6 us
    psum x1, waiting for transfers between devices, body(): lax.psum((shares[0], shares[1], shares[2]), 'seg')  56 us
    ppermute x2, starting transfers between devices, shifted(): return lax.ppermute(block, axis, route)  38.4 us
  transfers between devices with their start and end apart: 7, of which 7 were waited for; matrix products, arithmetic and copies ran while one was open for 1% of the time, Pallas kernels for 0%

commit v1 on v0

--- a/solution.py
+++ b/solution.py
@@ -87,7 +87,9 @@
 
 def body(starts, targets, counts, w_in, b_in, w_out):
     full_in, full_out = (
-        lax.all_gather(w_in, "batch", axis=0, tiled=True),
+        jnp.concatenate(
+            lax.all_to_all(jnp.stack([w_in] * lax.axis_size("batch")), "batch", 0, 0), axis=0
+        ),
         lax.all_gather(w_out, "batch", axis=0, tiled=True),
     )
     start_now = starts[0]

time: 729 us -> 673 us (0.923)
  waiting for transfers between devices: 472 us -> 405 us
  starting transfers between devices: 38.6 us -> 48.3 us
    all_gather x1 -> x0, waiting for transfers between devices: 73.6 us -> none  [body(): lax.all_gather(w_in, 'batch', axis=0, tiled=True)]
    all_to_all x0 -> x1, waiting for transfers between devices: none -> 28.3 us  [body(): lax.all_to_all(jnp.stack([w_in] * lax.axis_size('batch')), 'batch', 0, 0)]
    all_gather x1, waiting for transfers between devices: 71.7 us -> 50.2 us  [body(): lax.all_gather(w_out, 'batch', axis=0, tiled=True)]
    all_to_all x0 -> x1, starting transfers between devices: none -> 11.3 us  [body(): lax.all_to_all(jnp.stack([w_in] * lax.axis_size('batch')), 'batch', 0, 0)]
where the time goes in v1:
time: 673 us; the launch traced here: 671 us
  waiting for transfers between devices  405 us (60%)
  blocking collectives  138 us (21%)
  starting transfers between devices  48.3 us (7%)
  matrix products  26.6 us (4%)
  local copies, waits for them, and re-layouts  21.5 us (3%)
  between operations  15.2 us (2%)
  other arithmetic  13.9 us (2%)
    reduce_scatter x1, waiting for transfers between devices, body(): lax.psum_scatter(scaled_out, 'batch', scatter_dimension=0, tiled=True)  192 us
    unnamed x1, blocking collectives  80.2 us
    reduce_scatter x1, waiting for transfers between devices, body(): lax.psum_scatter(scaled_in, 'batch', scatter_dimension=0, tiled=True)  62.5 us
    psum x1, blocking collectives, body(): lax.psum((shares[0], shares[1], shares[2]), 'seg')  58.2 us
    psum x1, waiting for transfers between devices, body(): lax.psum((shares[0], shares[1], shares[2]), 'seg')  56.1 us
    all_gather x1, waiting for transfers between devices, body(): lax.all_gather(w_out, 'batch', axis=0, tiled=True)  50.2 us
    ppermute x2, starting transfers between devices, shifted(): return lax.ppermute(block, axis, route)  36.8 us
    all_to_all x1, waiting for transfers between devices, body(): lax.all_to_all(jnp.stack([w_in] * lax.axis_size('batch')), 'batch', 0, 0)  28.3 us
  transfers between devices with their start and end apart: 7, of which 7 were waited for; matrix products, arithmetic and copies ran while one was open for 1% of the time, Pallas kernels for 0%

profile of v1, /device:TPU:1, one launch (start us, length us, event | category | flops | bytes accessed | tf_op | source)
XLA Modules:
  0.0 671.3 jit_solution(4530539794999310874)
XLA Ops:
  7.9 2.4 stack.86
  10.3 11.3 %all-to-all-start = ((bf16[32,32,1024]{2,1,0:T(8,128)(2,1)}), bf16[32,32,1024]{2,1,0:T(8,128)(2,1)S(1)}, u32[]{:S(2)}, u32[]{:S(2)}) async-start(bf16[32,32,1024]{2,1,0:T(8,128)(2,1)} %stack.86), calls=%async_computation | async-start | bytes 4194304 | tf_op jit(solution)/shard_map/all_to_all | solution.py:91
  22.5 28.3 %all-to-all-done = bf16[32,32,1024]{2,1,0:T(8,128)(2,1)S(1)} async-done(((bf16[32,32,1024]{2,1,0:T(8,128)(2,1)}), bf16[32,32,1024]{2,1,0:T(8,128)(2,1)S(1)}, u32[]{:S(2)}, u32[]{:S(2)}) %all-to-all-start) | async-done | bytes 2097184 | tf_op jit(solution)/shard_map/all_to_all | solution.py:91
  50.8 50.2 %all-gather.2.cloned.1.call-done = bf16[1024,1024]{1,0:T(8,128)(2,1)} async-done(((bf16[32,1024]{1,0:T(8,128)(2,1)}), bf16[1024,1024]{1,0:T(8,128)(2,1)}) %all-gather.2.cloned.1.call-update) | async-done | bytes 2097168 | tf_op jit(solution)/shard_map/all_gather | solution.py:93
  100.9 1.4 broadcast_in_dim.14
  102.3 15.7 %while.30 = (s32[]{:T(128)}, f32[128,1024]{1,0:T(8,128)}, f32[3,128,1024]{2,1,0:T(8,128)}, s32[]{:T(128)}, bf16[1024,1024]{1,0:T(8,128)(2,1)S(1)}, /*index=5*/f3...) while((s32[]{:T(128)}, f32[128,1024]{1,0:T(8,128)}, ...), condition=%wide.region_1.2_spmd, body=%wide.region_0.1_spmd.sunk | while | flops 2150760448 | bytes 25706640 | solution.py:109
  104.0 2.4 fusion.174
  106.4 3.2 fusion.175
  109.5 3.3 fusion.176
  113.7 3.6 fusion.177
  118.0 34.9 %collective-permute-start = (f32[128,1024]{1,0:T(8,128)}, f32[128,1024]{1,0:T(8,128)S(1)}, u32[]{:S(2)}, u32[]{:S(2)}) collective-permute-start(f32[128,1024]{1,0:T(8,128)} %get-tuple-element.170), channel_id=1, source_target_pairs={{0,32},{32,64},{64,96},{1,33},{33,65},{65,97},{2,34},{34,66},{66,9... | collective-permute-start | bytes 1572872 | tf_op jit(solution)/shard_map/ppermute | solution.py:16
  152.9 6.4 collective-permute-done
  160.4 1.9 collective-permute-start.1
  163.0 8.7 %collective-permute-done.1 = f32[128,1024]{1,0:T(8,128)} collective-permute-done((f32[128,1024]{1,0:T(8,128)S(1)}, f32[128,1024]{1,0:T(8,128)}, u32[]{:S(2)}, u32[]{:S(2)}) %collective-permute-start.1) | collective-permute-done | bytes 524320 | tf_op jit(solution)/shard_map/ppermute | solution.py:16
  171.7 1.5 fusion.66
  173.1 2.5 broadcast.47.clone
  175.6 2.5 broadcast.47
  178.1 21.9 %while.31 = (s32[]{:T(128)}, f32[128,1024]{1,0:T(8,128)S(1)}, f32[1024,1024]{1,0:T(8,128)}, f32[1024,1024]{1,0:T(8,128)}, f32[1024]{0:T(1024)S(1)}, /*index=5*/s...) while((s32[]{:T(128)}, f32[128,1024]{1,0:T(8,128)S(1)}, ...), condition=%wide.region_7.8_spmd, body=%wide.region_2.7_spmd.sunk | while | flops 6195249152 | bytes 161800576 | solution.py:138
  179.0 1.2 dynamic-slice_convert_fusion.2
  180.3 1.5 fusion.211
  193.2 1.4 convolution_add_fusion.14
  195.4 1.4 convolution_add_fusion.15
  197.4 2.0 copy-done.2
  200.0 5.0 broadcast_multiply_fusion.1
  205.1 5.0 broadcast_multiply_fusion
  212.0 80.2 %all-reduce = f32[1024]{0:T(1024)S(1)} all-reduce(f32[1024]{0:T(1024)S(1)} %broadcast_multiply_fusion.2), channel_id=4, replica_groups=mesh['seg'=4,'batch'=32] {'batch'}, use_global_device_ids=true, to_apply=%region_12.13.clone | all-reduce | flops 1024 | bytes 8192
  292.2 58.2 %psum.23 = f32[32]{0:T(128)} all-reduce(f32[32]{0:T(128)S(1)} %dynamic-slice.1), channel_id=1, replica_groups=mesh['seg'=4,'batch'=32] {'seg'}, use_global_device_ids=true, to_apply=%region_13.14 | all-reduce | flops 32 | bytes 256 | tf_op jit(solution)/shard_map/psum | solution.py:150
  350.4 62.5 %reduce-scatter.3.cloned.1.call-done = f32[32,1024]{1,0:T(8,128)} async-done(((f32[1024,1024]{1,0:T(8,128)}), f32[32,1024]{1,0:T(8,128)}) %reduce-scatter.3.cloned.1.call-update) | async-done | bytes 131088 | tf_op jit(solution)/shard_map/reduce_scatter | solution.py:146
  413.0 191.6 %reduce-scatter.5.cloned.1.call-done = f32[32,1024]{1,0:T(8,128)} async-done(((f32[1024,1024]{1,0:T(8,128)}), f32[32,1024]{1,0:T(8,128)}) %reduce-scatter.5.cloned.1.call-update) | async-done | bytes 131088 | tf_op jit(solution)/shard_map/reduce_scatter | solution.py:147
  605.5 56.1 %all-reduce.4.cloned.1.call-done = (f32[32,1024]{1,0:T(8,128)}, f32[32,1024]{1,0:T(8,128)}) async-done(((f32[32,1024]{1,0:T(8,128)}, f32[32,1024]{1,0:T(8,128)}), (f32[32,1024]{1,0:T(8,128)}, f32[32,1024]{1,0:T(8,128)})) %all-reduce.4.cloned.1.call-update) | async-done | bytes 262160 | tf_op jit(solution)/shard_map/psum | solution.py:150
  661.6 1.6 copy.40
  663.2 1.6 copy.41
  (54 shorter events, 19.4 us)
Async XLA Ops:
  7.2 93.8 %all-gather.2.cloned.1.call-start = ((), (), s32[]{:S(2)}) async-start(), calls=%async_computation.3 | async-start | bytes 2162688 | tf_op jit(solution)/shard_map/all_gather | solution.py:93
  10.3 11.4 %copy-start.7 = (f32[1,128,1024]{2,1,0:T(8,128)S(1)}, f32[1,128,1024]{2,1,0:T(8,128)}, u32[]{:S(2)}) copy-start(f32[1,128,1024]{2,1,0:T(8,128)} %param.10) | copy-start | bytes 1572868
  10.3 40.4 %all-to-all-start = ((bf16[32,32,1024]{2,1,0:T(8,128)(2,1)}), bf16[32,32,1024]{2,1,0:T(8,128)(2,1)S(1)}, u32[]{:S(2)}, u32[]{:S(2)}) async-start(bf16[32,32,1024]{2,1,0:T(8,128)(2,1)} %stack.86), calls=%async_computation | async-start | bytes 4194304 | tf_op jit(solution)/shard_map/all_to_all | solution.py:91
  21.6 80.7 %copy-start.6 = (f32[1024]{0:T(1024)S(1)}, f32[1024]{0:T(1024)}, u32[]{:S(2)}) copy-start(f32[1024]{0:T(1024)} %param.14) | copy-start | bytes 12292
  21.6 391.3 %reduce-scatter.3.cloned.1.call-start = ((), (), s32[]{:S(2)}) async-start(), calls=%async_computation.4 | async-start | bytes 4325376 | tf_op jit(solution)/shard_map/reduce_scatter | solution.py:146
  118.0 41.3 %collective-permute-start = (f32[128,1024]{1,0:T(8,128)}, f32[128,1024]{1,0:T(8,128)S(1)}, u32[]{:S(2)}, u32[]{:S(2)}) collective-permute-start(f32[128,1024]{1,0:T(8,128)} %get-tuple-element.170), channel_id=1, source_target_pairs={{0,32},{32,64},{64,96},{1,33},{33,65},{65,97},{2,34},{34,66},{66,9... | collective-permute-start | bytes 1572872 | tf_op jit(solution)/shard_map/ppermute | solution.py:16
  160.4 11.2 %collective-permute-start.1 = (f32[128,1024]{1,0:T(8,128)S(1)}, f32[128,1024]{1,0:T(8,128)}, u32[]{:S(2)}, u32[]{:S(2)}) collective-permute-start(f32[128,1024]{1,0:T(8,128)S(1)} %subtract_multiply_fusion), channel_id=1, source_target_pairs={{32,0},{64,32},{96,64},{33,1},{65,33},{97,65},{34,2},{66,34},{98,6... | collective-permute-start | bytes 1572872 | tf_op jit(solution)/shard_map/ppermute | solution.py:16
  179.0 2.8 copy-start
  179.0 2.8 copy-start.5
  191.1 2.2 copy-start.3
  193.2 2.2 copy-start.1
  195.4 2.0 copy-start.4
  197.4 2.0 copy-start.2
  205.0 399.6 %reduce-scatter.5.cloned.1.call-start = ((), (), s32[]{:S(2)}) async-start(), calls=%async_computation.5 | async-start | bytes 4325376 | tf_op jit(solution)/shard_map/reduce_scatter | solution.py:147
  210.1 0.7 copy-start.8
  210.1 451.5 %all-reduce.4.cloned.1.call-start = ((), (), s32[]{:S(2)}) async-start(), calls=%async_computation.6 | async-start | bytes 524288 | tf_op jit(solution)/shard_map/psum | solution.py:150
Sparse Core Ops, SparseCore 0:
  11.1 89.8 all-gather.1
  205.1 207.7 reduce-scatter.2
  415.4 189.2 reduce-scatter.4
  607.0 54.5 all-reduce.3
